TPU v7x, 256 devices: a whole 4x4x8 slice. The times are simulated.
256 devices in a mesh: seq: 32 (over x, z), head: 8 (over y, core).
Axes of the slice: x: 4, y: 4, z: 8, core: 2. Of those that a mesh axis runs over, the one named last changes fastest.
Arguments:
- tokens: bfloat16 [8192, 3072], P('seq', 'head'), may hold values from -6 to 6
- norm_gain: float32 [3072], replicated, may hold values from 0.1 to 1.9
- w_query: bfloat16 [3072, 3072], P(None, 'head'), may hold values from -0.109375 to 0.109375
- w_key: bfloat16 [3072, 1024], P(None, 'head'), may hold values from -0.3125 to 0.3125
- w_value: bfloat16 [3072, 1024], P(None, 'head'), may hold values from -0.109375 to 0.109375
- w_out: bfloat16 [3072, 3072], P('head'), may hold values from -0.109375 to 0.109375
- keys_cache: bfloat16 [65536, 1024], P('seq', 'head'), may hold values from -120 to 120
- values_cache: bfloat16 [65536, 1024], P('seq', 'head'), may hold values from -6 to 6
- cached_lengths: int32 [4], replicated, may hold values from 0 to 14336, as said below
- rope_offsets: int32 [4], replicated, may hold values from 0 to 8191
Outputs:
- attn_proj: bfloat16 [8192, 3072], P('seq', 'head')
- keys_updated: bfloat16 [65536, 1024], P('seq', 'head')
- values_updated: bfloat16 [65536, 1024], P('seq', 'head')
Inputs may be any that keep to these rules, and one draw needn't show every extreme that they name: `cached_lengths`: in every draw one request has exactly 14336 cached tokens.
All inputs are finite; a program needn't handle non-finite values.
Results may differ from a plain program's by a relative error of at most 0.02.
Values may be sent and summed in bfloat16 or wider, within the bound.
A program may use at most 128 MiB of HBM per device.

v0:
```python
import math
import jax
import jax.numpy as jnp
from jax import lax
from jax.sharding import PartitionSpec as P

HD = 128
rope_base = 500000.0
neg_large = -1e30


def shifted(shard, axis, by):
    devices = lax.axis_size(axis)
    return lax.ppermute(shard, axis, [(i, (i + by) % devices) for i in range(devices)])


def rotate(vectors, positions):
    half_width = vectors.shape[-1] // 2
    frequency = rope_base ** (-jnp.arange(half_width, dtype=jnp.float32) * 2.0 / vectors.shape[-1])
    angles = positions.astype(jnp.float32)[:, None] * frequency[None, :]
    cosine = jnp.cos(angles)[:, None, :]
    sine_part = jnp.sin(angles)[:, None, :]
    first_half = vectors[..., :half_width]
    second_half = vectors[..., half_width:]
    return jnp.concatenate(
        [
            first_half * cosine - second_half * sine_part,
            second_half * cosine + first_half * sine_part,
        ],
        -1,
    )


def shards(
    tokens,
    norm_gain,
    w_query,
    w_key,
    w_value,
    w_out,
    keys_cache,
    values_cache,
    cached_lengths,
    rope_offsets,
):
    gathered = lax.all_gather(tokens, "head", axis=1, tiled=True)
    row_count = gathered.shape[0]
    requests = cached_lengths.shape[0]
    groups = lax.axis_size("seq") // requests
    member = lax.axis_index("seq")
    request = member % requests
    position_in = member // requests
    length = lax.dynamic_index_in_dim(cached_lengths, request, 0, False)
    offset = lax.dynamic_index_in_dim(rope_offsets, request, 0, False)
    widened = gathered.astype(jnp.float32)
    normed = (
        widened * lax.rsqrt(jnp.mean(widened * widened, -1, keepdims=True) + 1e-05) * norm_gain
    ).astype(jnp.bfloat16)
    index_new = position_in * row_count + jnp.arange(row_count, dtype=jnp.int32)
    positions = offset + length + index_new
    kv_heads = w_key.shape[1] // HD
    q_heads = w_query.shape[1] // HD
    repeat = q_heads // kv_heads
    queries = rotate(
        jnp.dot(normed, w_query, preferred_element_type=jnp.float32).reshape(
            row_count, q_heads, HD
        ),
        positions,
    ).astype(jnp.bfloat16)
    new_keys = (
        rotate(
            jnp.dot(normed, w_key, preferred_element_type=jnp.float32).reshape(
                row_count, kv_heads, HD
            ),
            positions,
        )
        .astype(jnp.bfloat16)
        .reshape(row_count, kv_heads * HD)
    )
    new_values = jnp.dot(normed, w_value, preferred_element_type=jnp.float32).astype(jnp.bfloat16)
    grouped = (
        queries.reshape(row_count, kv_heads, repeat, HD)
        .transpose(1, 2, 0, 3)
        .reshape(kv_heads, repeat * row_count, HD)
    )
    slab_rows = keys_cache.shape[0]
    score_scale = 1.0 / math.sqrt(HD)

    def attend(softmax_state, query_group, key_block, value_block, visible):
        running_max, denominator, accumulated = softmax_state
        scores = (
            jnp.einsum(
                "gqd,kgd->gqk",
                query_group,
                key_block.reshape(-1, kv_heads, HD),
                preferred_element_type=jnp.float32,
            )
            * score_scale
        )
        masked = jnp.where(visible, scores, neg_large)
        new_max = jnp.maximum(running_max, jnp.max(masked, -1))
        weights = jnp.where(visible, jnp.exp(masked - new_max[..., None]), 0.0)
        factor = jnp.exp(running_max - new_max)
        denominator = denominator * factor + jnp.sum(weights, -1)
        accumulated = accumulated * factor[..., None] + jnp.einsum(
            "gqk,kgd->gqd",
            weights.astype(jnp.bfloat16),
            value_block.reshape(-1, kv_heads, HD),
            preferred_element_type=jnp.float32,
        )
        return (new_max, denominator, accumulated)

    def attend_pair(
        softmax_state,
        query_anchor,
        query_group,
        slab_keys,
        slab_values,
        slab_source,
        fresh_keys,
        fresh_values,
        fresh_source,
    ):
        query_index = jnp.tile(
            query_anchor * row_count + jnp.arange(row_count, dtype=jnp.int32), repeat
        )
        slots = slab_source * slab_rows + jnp.arange(slab_rows, dtype=jnp.int32)
        old_visible = (slots < length)[None, None, :]
        fresh_index = fresh_source * row_count + jnp.arange(row_count, dtype=jnp.int32)
        fresh_visible = (fresh_index[None, :] <= query_index[:, None])[None]
        softmax_state = attend(softmax_state, query_group, slab_keys, slab_values, old_visible)
        softmax_state = attend(softmax_state, query_group, fresh_keys, fresh_values, fresh_visible)
        return softmax_state

    def write_fresh(out_keys, out_values, fresh_keys, fresh_values, fresh_source):
        fresh_index = fresh_source * row_count + jnp.arange(row_count, dtype=jnp.int32)
        local_slot = length + fresh_index - position_in * slab_rows
        target = jnp.where((local_slot >= 0) & (local_slot < slab_rows), local_slot, slab_rows)
        out_keys = out_keys.at[target].set(fresh_keys, mode="drop")
        out_values = out_values.at[target].set(fresh_values, mode="drop")
        return (out_keys, out_values)

    def absorb(loop_carry, incoming, source):
        softmax_state, out_keys, out_values = loop_carry
        fresh_keys = incoming[0, slab_rows:]
        fresh_values = incoming[1, slab_rows:]
        softmax_state = attend_pair(
            softmax_state,
            position_in,
            grouped,
            incoming[0, :slab_rows],
            incoming[1, :slab_rows],
            source,
            fresh_keys,
            fresh_values,
            source,
        )
        out_keys, out_values = write_fresh(out_keys, out_values, fresh_keys, fresh_values, source)
        return (softmax_state, out_keys, out_values)

    start_state = (
        jnp.full((kv_heads, repeat * row_count), neg_large, jnp.float32),
        jnp.zeros((kv_heads, repeat * row_count), jnp.float32),
        jnp.zeros((kv_heads, repeat * row_count, HD), jnp.float32),
    )
    outgoing = jnp.stack(
        [
            jnp.concatenate([keys_cache, new_keys], 0),
            jnp.concatenate([values_cache, new_values], 0),
        ],
        0,
    )
    loop_carry = absorb((start_state, keys_cache, values_cache), outgoing, position_in)

    def cycle_step(cycle_turn, cycle_carry):
        held_blocks, inner_carry = cycle_carry
        held_blocks = shifted(held_blocks, "seq", requests)
        source = (position_in - cycle_turn) % groups
        return (held_blocks, absorb(inner_carry, held_blocks, source))

    unused, loop_carry = lax.fori_loop(1, groups, cycle_step, (outgoing, loop_carry))
    final_state, keys_updated, values_updated = loop_carry
    running_max, denominator, accumulated = final_state
    attended = (
        (accumulated / denominator[..., None])
        .reshape(kv_heads, repeat, row_count, HD)
        .transpose(2, 0, 1, 3)
        .reshape(row_count, q_heads * HD)
        .astype(jnp.bfloat16)
    )
    partial_value = jnp.dot(attended, w_out, preferred_element_type=jnp.float32)
    summed = lax.psum(partial_value.astype(jnp.bfloat16), "head").astype(jnp.float32)
    share_width = partial_value.shape[1] // lax.axis_size("head")
    projected = lax.dynamic_slice_in_dim(
        summed, lax.axis_index("head") * share_width, share_width, 1
    )
    return (projected.astype(jnp.bfloat16), keys_updated, values_updated)


def solution(mesh):
    return jax.shard_map(
        shards,
        mesh=mesh,
        in_specs=(
            P("seq", "head"),
            P(),
            P(None, "head"),
            P(None, "head"),
            P(None, "head"),
            P("head", None),
            P("seq", "head"),
            P("seq", "head"),
            P(),
            P(),
        ),
        out_specs=(P("seq", "head"), P("seq", "head"), P("seq", "head")),
        check_vma=False,
    )
```

profile of v0, /device:TPU:2, one launch (start us, length us, event | category | flops | bytes accessed | tf_op | source)
XLA Modules:
  0.0 639.8 jit_solution(14705658243390205139)
XLA Ops:
  8.4 2.1 copy.53
  17.2 23.6 %all-gather.2.cloned.1.call-done = bf16[256,3072]{1,0:T(8,128)(2,1)} async-done(((bf16[256,384]{1,0:T(8,128)(2,1)}), bf16[256,3072]{1,0:T(8,128)(2,1)}) %all-gather.2.cloned.1.call-update) | async-done | bytes 1572880 | tf_op jit(solution)/shard_map/all_gather | solution.py:46
  40.8 1.8 fusion.40
  43.2 2.4 convolution_bitcast_fusion.1
  46.1 2.3 convolution_convert_fusion.1
  49.5 3.2 scatter_custom_fusion.2
  53.9 3.2 scatter_custom_fusion.3
  57.1 3.3 fusion.81
  61.2 1.8 copy.20
  63.0 2.1 fusion.37
  66.3 1.6 fusion.39
  71.4 386.1 %while.25 = (s32[]{:T(128)}, bf16[2,2304,128]{2,1,0:T(8,128)(2,1)}, f32[1,768]{1,0:T(1,128)S(1)}, f32[1,768]{1,0:T(1,128)}, f32[1,768,128]{2,1,0:T(8,128)}, /*in...) while((s32[]{:T(128)}, bf16[2,2304,128]{2,1,0:T(8,128)(2,1)}, ...), condition=%wide.region_14.15_spmd, body=%wide.region_7.14_spmd.sunk | while | flops 929181184 | bytes 57951692 | solution.py:181
  71.4 5.7 collective-permute-start
  79.0 41.7 %collective-permute-done = bf16[2,2304,128]{2,1,0:T(8,128)(2,1)S(1)} collective-permute-done((bf16[2,2304,128]{2,1,0:T(8,128)(2,1)}, bf16[2,2304,128]{2,1,0:T(8,128)(2,1)S(1)}, u32[]{:S(2)}, u32[]{:S(2)}) %collective-permute-start) | collective-permute-done | bytes 1179680 | tf_op jit(solution)/shard_map/while/body/eval_jaxpr/ppermute | solution.py:14
  120.7 2.1 fusion.105
  125.4 1.6 fusion.108
  129.5 3.2 scatter_custom_fusion.14
  132.7 3.2 scatter_custom_fusion.15
  135.8 5.2 fusion.109
  141.0 5.1 collective-permute-start
  148.0 23.2 %collective-permute-done = bf16[2,2304,128]{2,1,0:T(8,128)(2,1)S(1)} collective-permute-done((bf16[2,2304,128]{2,1,0:T(8,128)(2,1)}, bf16[2,2304,128]{2,1,0:T(8,128)(2,1)S(1)}, u32[]{:S(2)}, u32[]{:S(2)}) %collective-permute-start) | collective-permute-done | bytes 1179680 | tf_op jit(solution)/shard_map/while/body/eval_jaxpr/ppermute | solution.py:14
  171.2 2.1 fusion.105
  175.9 1.6 fusion.108
  180.0 3.2 scatter_custom_fusion.14
  183.2 3.2 scatter_custom_fusion.15
  186.4 5.2 fusion.109
  191.5 4.2 collective-permute-start
  197.6 27.7 %collective-permute-done = bf16[2,2304,128]{2,1,0:T(8,128)(2,1)S(1)} collective-permute-done((bf16[2,2304,128]{2,1,0:T(8,128)(2,1)}, bf16[2,2304,128]{2,1,0:T(8,128)(2,1)S(1)}, u32[]{:S(2)}, u32[]{:S(2)}) %collective-permute-start) | collective-permute-done | bytes 1179680 | tf_op jit(solution)/shard_map/while/body/eval_jaxpr/ppermute | solution.py:14
  225.3 2.1 fusion.105
  230.1 1.6 fusion.108
  234.1 3.2 scatter_custom_fusion.14
  237.3 3.2 scatter_custom_fusion.15
  240.5 5.2 fusion.109
  245.7 1.6 collective-permute-start
  249.1 29.3 %collective-permute-done = bf16[2,2304,128]{2,1,0:T(8,128)(2,1)S(1)} collective-permute-done((bf16[2,2304,128]{2,1,0:T(8,128)(2,1)}, bf16[2,2304,128]{2,1,0:T(8,128)(2,1)S(1)}, u32[]{:S(2)}, u32[]{:S(2)}) %collective-permute-start) | collective-permute-done | bytes 1179680 | tf_op jit(solution)/shard_map/while/body/eval_jaxpr/ppermute | solution.py:14
  278.4 2.1 fusion.105
  283.2 1.6 fusion.108
  287.2 3.2 scatter_custom_fusion.14
  290.4 3.2 scatter_custom_fusion.15
  293.6 5.2 fusion.109
  298.8 2.8 collective-permute-start
  303.4 27.8 %collective-permute-done = bf16[2,2304,128]{2,1,0:T(8,128)(2,1)S(1)} collective-permute-done((bf16[2,2304,128]{2,1,0:T(8,128)(2,1)}, bf16[2,2304,128]{2,1,0:T(8,128)(2,1)S(1)}, u32[]{:S(2)}, u32[]{:S(2)}) %collective-permute-start) | collective-permute-done | bytes 1179680 | tf_op jit(solution)/shard_map/while/body/eval_jaxpr/ppermute | solution.py:14
  331.2 2.1 fusion.105
  336.0 1.6 fusion.108
  340.0 3.2 scatter_custom_fusion.14
  343.2 3.2 scatter_custom_fusion.15
  346.4 5.2 fusion.109
  351.5 3.2 collective-permute-start
  356.7 27.8 %collective-permute-done = bf16[2,2304,128]{2,1,0:T(8,128)(2,1)S(1)} collective-permute-done((bf16[2,2304,128]{2,1,0:T(8,128)(2,1)}, bf16[2,2304,128]{2,1,0:T(8,128)(2,1)S(1)}, u32[]{:S(2)}, u32[]{:S(2)}) %collective-permute-start) | collective-permute-done | bytes 1179680 | tf_op jit(solution)/shard_map/while/body/eval_jaxpr/ppermute | solution.py:14
  384.5 2.1 fusion.105
  389.3 1.6 fusion.108
  393.3 3.2 scatter_custom_fusion.14
  396.5 3.2 scatter_custom_fusion.15
  399.7 5.2 fusion.109
  404.8 2.6 collective-permute-start
  409.3 27.8 %collective-permute-done = bf16[2,2304,128]{2,1,0:T(8,128)(2,1)S(1)} collective-permute-done((bf16[2,2304,128]{2,1,0:T(8,128)(2,1)}, bf16[2,2304,128]{2,1,0:T(8,128)(2,1)S(1)}, u32[]{:S(2)}, u32[]{:S(2)}) %collective-permute-start) | collective-permute-done | bytes 1179680 | tf_op jit(solution)/shard_map/while/body/eval_jaxpr/ppermute | solution.py:14
  437.1 2.1 fusion.105
  441.9 1.6 fusion.108
  445.9 3.2 scatter_custom_fusion.14
  449.1 3.2 scatter_custom_fusion.15
  452.3 5.2 fusion.109
  459.5 2.2 convolution_convert_fusion
  461.7 169.6 %all-reduce.2.cloned.1.call-done = bf16[256,3072]{1,0:T(8,128)(2,1)} async-done(((bf16[256,3072]{1,0:T(8,128)(2,1)}), bf16[256,3072]{1,0:T(8,128)(2,1)}) %all-reduce.2.cloned.1.call-update) | async-done | bytes 1572880 | tf_op jit(solution)/shard_map/psum | solution.py:192
  631.3 1.6 convert_convert_fusion
  (179 shorter events, 66.0 us)
Async XLA Ops:
  7.2 452.3 %copy-start = (bf16[384,3072]{1,0:T(8,128)(2,1)S(1)}, bf16[384,3072]{1,0:T(8,128)(2,1)}, u32[]{:S(2)}) copy-start(bf16[384,3072]{1,0:T(8,128)(2,1)} %param.17) | copy-start | bytes 7077892
  7.2 36.1 %copy-start.9 = (f32[3072]{0:T(1024)S(1)}, f32[3072]{0:T(1024)}, u32[]{:S(2)}) copy-start(f32[3072]{0:T(1024)} %param.13) | copy-start | bytes 36868
  7.2 33.6 %all-gather.2.cloned.1.call-start = ((), (), s32[]{:S(2)}) async-start(), calls=%async_computation | async-start | bytes 1769472 | tf_op jit(solution)/shard_map/all_gather | solution.py:46
  8.4 37.7 %copy-start.2 = (bf16[2048,128]{1,0:T(8,128)(2,1)}, bf16[2048,128]{1,0:T(8,128)(2,1)S(1)}, u32[]{:S(2)}) copy-start(bf16[2048,128]{1,0:T(8,128)(2,1)S(1)} %copy.52) | copy-start | bytes 1572868
  10.5 620.8 %all-reduce.2.cloned.1.call-start = ((), (), s32[]{:S(2)}) async-start(), calls=%async_computation.1 | async-start | bytes 3145728 | tf_op jit(solution)/shard_map/psum | solution.py:192
  42.6 0.6 copy-start.7
  48.4 8.6 %copy-start.8 = (f32[256]{0:T(256)S(1)}, f32[256]{0:T(256)}, u32[]{:S(2)}) copy-start(f32[256]{0:T(256)} %copy-done.7) | copy-start | bytes 3076
  57.1 3.4 copy-start.3
  57.1 3.4 copy-start.4
  71.4 49.3 %collective-permute-start = (bf16[2,2304,128]{2,1,0:T(8,128)(2,1)}, bf16[2,2304,128]{2,1,0:T(8,128)(2,1)S(1)}, u32[]{:S(2)}, u32[]{:S(2)}) collective-permute-start(bf16[2,2304,128]{2,1,0:T(8,128)(2,1)} %get-tuple-element.428), channel_id=1, source_target_pairs={{0,32},{8,40},{16,48},{24,56},{32,64},{40,72},{48,80},{56,88},{64,... | collective-permute-start | bytes 3538952 | tf_op jit(solution)/shard_map/while/body/eval_jaxpr/ppermute | solution.py:14
  122.8 4.2 copy-start.1
  125.4 1.8 copy-start.5
  127.3 1.2 copy-start.6
  141.0 30.2 %collective-permute-start = (bf16[2,2304,128]{2,1,0:T(8,128)(2,1)}, bf16[2,2304,128]{2,1,0:T(8,128)(2,1)S(1)}, u32[]{:S(2)}, u32[]{:S(2)}) collective-permute-start(bf16[2,2304,128]{2,1,0:T(8,128)(2,1)} %get-tuple-element.428), channel_id=1, source_target_pairs={{0,32},{8,40},{16,48},{24,56},{32,64},{40,72},{48,80},{56,88},{64,... | collective-permute-start | bytes 3538952 | tf_op jit(solution)/shard_map/while/body/eval_jaxpr/ppermute | solution.py:14
  173.3 4.2 copy-start.1
  175.9 1.8 copy-start.5
  177.8 1.2 copy-start.6
  191.5 33.8 %collective-permute-start = (bf16[2,2304,128]{2,1,0:T(8,128)(2,1)}, bf16[2,2304,128]{2,1,0:T(8,128)(2,1)S(1)}, u32[]{:S(2)}, u32[]{:S(2)}) collective-permute-start(bf16[2,2304,128]{2,1,0:T(8,128)(2,1)} %get-tuple-element.428), channel_id=1, source_target_pairs={{0,32},{8,40},{16,48},{24,56},{32,64},{40,72},{48,80},{56,88},{64,... | collective-permute-start | bytes 3538952 | tf_op jit(solution)/shard_map/while/body/eval_jaxpr/ppermute | solution.py:14
  227.4 4.2 copy-start.1
  230.1 1.8 copy-start.5
  231.9 1.2 copy-start.6
  245.7 32.8 %collective-permute-start = (bf16[2,2304,128]{2,1,0:T(8,128)(2,1)}, bf16[2,2304,128]{2,1,0:T(8,128)(2,1)S(1)}, u32[]{:S(2)}, u32[]{:S(2)}) collective-permute-start(bf16[2,2304,128]{2,1,0:T(8,128)(2,1)} %get-tuple-element.428), channel_id=1, source_target_pairs={{0,32},{8,40},{16,48},{24,56},{32,64},{40,72},{48,80},{56,88},{64,... | collective-permute-start | bytes 3538952 | tf_op jit(solution)/shard_map/while/body/eval_jaxpr/ppermute | solution.py:14
  280.5 4.2 copy-start.1
  283.2 1.8 copy-start.5
  285.0 1.2 copy-start.6
  298.8 32.5 %collective-permute-start = (bf16[2,2304,128]{2,1,0:T(8,128)(2,1)}, bf16[2,2304,128]{2,1,0:T(8,128)(2,1)S(1)}, u32[]{:S(2)}, u32[]{:S(2)}) collective-permute-start(bf16[2,2304,128]{2,1,0:T(8,128)(2,1)} %get-tuple-element.428), channel_id=1, source_target_pairs={{0,32},{8,40},{16,48},{24,56},{32,64},{40,72},{48,80},{56,88},{64,... | collective-permute-start | bytes 3538952 | tf_op jit(solution)/shard_map/while/body/eval_jaxpr/ppermute | solution.py:14
  333.3 4.2 copy-start.1
  336.0 1.8 copy-start.5
  337.8 1.2 copy-start.6
  351.5 33.0 %collective-permute-start = (bf16[2,2304,128]{2,1,0:T(8,128)(2,1)}, bf16[2,2304,128]{2,1,0:T(8,128)(2,1)S(1)}, u32[]{:S(2)}, u32[]{:S(2)}) collective-permute-start(bf16[2,2304,128]{2,1,0:T(8,128)(2,1)} %get-tuple-element.428), channel_id=1, source_target_pairs={{0,32},{8,40},{16,48},{24,56},{32,64},{40,72},{48,80},{56,88},{64,... | collective-permute-start | bytes 3538952 | tf_op jit(solution)/shard_map/while/body/eval_jaxpr/ppermute | solution.py:14
  386.6 4.2 copy-start.1
  389.3 1.8 copy-start.5
  391.1 1.2 copy-start.6
  404.8 32.3 %collective-permute-start = (bf16[2,2304,128]{2,1,0:T(8,128)(2,1)}, bf16[2,2304,128]{2,1,0:T(8,128)(2,1)S(1)}, u32[]{:S(2)}, u32[]{:S(2)}) collective-permute-start(bf16[2,2304,128]{2,1,0:T(8,128)(2,1)} %get-tuple-element.428), channel_id=1, source_target_pairs={{0,32},{8,40},{16,48},{24,56},{32,64},{40,72},{48,80},{56,88},{64,... | collective-permute-start | bytes 3538952 | tf_op jit(solution)/shard_map/while/body/eval_jaxpr/ppermute | solution.py:14
  439.2 4.2 copy-start.1
  441.9 1.8 copy-start.5
  443.7 1.2 copy-start.6
Sparse Core Ops, SparseCore 0:
  10.6 30.1 all-gather.1
  461.8 169.4 all-reduce.1
where the time goes:
time: 642 us; the launch traced here: 640 us
  waiting for transfers between devices  399 us (62%)
  matrix products  84.8 us (13%)
  local copies, waits for them, and re-layouts  67 us (10%)
  other arithmetic  48 us (7%)
  starting transfers between devices  25.4 us (4%)
  between operations  15.5 us (2%)
    ppermute x7, waiting for transfers between devices, shifted(): lax.ppermute(shard, axis, [(i, (i + by) % devices) for i in range(devices)])  205 us
    psum x1, waiting for transfers between devices, shards(): lax.psum(partial_value.astype(jnp.bfloat16), 'head').astype(jnp.float32)  170 us
    dot_general x16, matrix products, attend(): jnp.einsum('gqk,kgd->gqd', weights.astype(jnp.bfloat16), value_block.resh...  46.8 us
    dot_general x16, matrix products, attend(): jnp.einsum('gqd,kgd->gqk', query_group, key_block.reshape(-1, kv_heads, H...  27.8 us
    scatter x8, local copies, waits for them, and re-layouts, write_fresh(): out_keys = out_keys.at[target].set(fresh_keys, mode='drop')  25.5 us
    scatter x8, local copies, waits for them, and re-layouts, write_fresh(): out_values = out_values.at[target].set(fresh_values, mode='drop')  25.5 us
    ppermute x7, starting transfers between devices, shifted(): lax.ppermute(shard, axis, [(i, (i + by) % devices) for i in range(devices)])  25.3 us
    all_gather x1, waiting for transfers between devices, shards(): gathered = lax.all_gather(tokens, 'head', axis=1, tiled=True)  23.6 us
  transfers between devices with their start and end apart: 9, of which 9 were waited for; matrix products, arithmetic and copies ran while one was open for 3% of the time, Pallas kernels for 0%

commit v1 on v0

--- a/solution.py
+++ b/solution.py
@@ -43,7 +43,13 @@
     cached_lengths,
     rope_offsets,
 ):
-    gathered = lax.all_gather(tokens, "head", axis=1, tiled=True)
+    fix_local_data = lambda raw, mesh_ax: jnp.concatenate(
+        jax.lax.all_to_all(
+            jnp.stack([raw for _ in range(jax.lax.axis_size(mesh_ax))], 0), mesh_ax, 0, 0
+        ),
+        1,
+    )
+    gathered = fix_local_data(tokens, mesh_ax="head")
     row_count = gathered.shape[0]
     requests = cached_lengths.shape[0]
     groups = lax.axis_size("seq") // requests

time: 642 us -> 673 us (1.048)
  waiting for transfers between devices: 399 us -> 413 us
  local copies, waits for them, and re-layouts: 67 us -> 75.5 us
  starting transfers between devices: 25.4 us -> 33.3 us
    ppermute x7, waiting for transfers between devices: 205 us -> 320 us  [shifted(): lax.ppermute(shard, axis, [(i, (i + by) % devices) for i in range(devices)])]
    psum x1, waiting for transfers between devices: 170 us -> 81.7 us  [shards(): lax.psum(partial_value.astype(jnp.bfloat16), 'head').astype(jnp.float32)]
    all_gather x1 -> x0, waiting for transfers between devices: 23.6 us -> none  [shards(): gathered = lax.all_gather(tokens, 'head', axis=1, tiled=True)]
    all_to_all x0 -> x1, waiting for transfers between devices: none -> 11.4 us  [shards(): jax.lax.all_to_all(jnp.stack([raw for _ in range(jax.lax.axis_size(mesh_a...]
where the time goes in v1:
time: 673 us; the launch traced here: 671 us
  waiting for transfers between devices  413 us (61%)
  matrix products  80.2 us (12%)
  local copies, waits for them, and re-layouts  75.5 us (11%)
  other arithmetic  52.6 us (8%)
  starting transfers between devices  33.3 us (5%)
  between operations  15.6 us (2%)
    ppermute x7, waiting for transfers between devices, shifted(): lax.ppermute(shard, axis, [(i, (i + by) % devices) for i in range(devices)])  320 us
    psum x1, waiting for transfers between devices, shards(): lax.psum(partial_value.astype(jnp.bfloat16), 'head').astype(jnp.float32)  81.7 us
    dot_general x16, matrix products, attend(): jnp.einsum('gqk,kgd->gqd', weights.astype(jnp.bfloat16), value_block.resh...  46.8 us
    ppermute x7, starting transfers between devices, shifted(): lax.ppermute(shard, axis, [(i, (i + by) % devices) for i in range(devices)])  28.8 us
    dot_general x16, matrix products, attend(): jnp.einsum('gqd,kgd->gqk', query_group, key_block.reshape(-1, kv_heads, H...  27.8 us
    scatter x8, local copies, waits for them, and re-layouts, write_fresh(): out_keys = out_keys.at[target].set(fresh_keys, mode='drop')  25.5 us
    scatter x8, local copies, waits for them, and re-layouts, write_fresh(): out_values = out_values.at[target].set(fresh_values, mode='drop')  25.5 us
    reduce_sum x16, other arithmetic, attend(): denominator = denominator * factor + jnp.sum(weights, -1)  14.2 us
  transfers between devices with their start and end apart: 9, of which 9 were waited for; matrix products, arithmetic and copies ran while one was open for 3% of the time, Pallas kernels for 0%

profile of v1, /device:TPU:2, one launch (start us, length us, event | category | flops | bytes accessed | tf_op | source)
XLA Modules:
  0.0 670.8 jit_solution(15033050906559809790)
XLA Ops:
  8.4 2.1 copy.67
  10.5 2.2 stack.8
  12.7 4.5 all-to-all-start
  18.5 4.3 copy.31
  27.5 11.4 %all-to-all-done = bf16[8,256,384]{2,1,0:T(8,128)(2,1)} async-done(((bf16[8,256,384]{2,1,0:T(8,128)(2,1)}), bf16[8,256,384]{2,1,0:T(8,128)(2,1)}, u32[]{:S(2)}, u32[]{:S(2)}) %all-to-all-start) | async-done | bytes 1572896 | tf_op jit(solution)/shard_map/all_to_all | solution.py:47
  38.9 2.6 copy.29
  41.5 1.9 multiply_reduce_fusion
  43.4 1.9 fusion.41
  47.4 2.2 convolution_convert_fusion.1
  50.7 3.2 scatter_custom_fusion.2
  55.1 3.2 scatter_custom_fusion.3
  58.3 2.0 multiply_convert_fusion
  62.0 1.8 copy.33
  63.8 2.1 fusion.37
  67.1 1.6 fusion.39
  72.2 504.3 %while.25 = (s32[]{:T(128)}, bf16[2,2304,128]{2,1,0:T(8,128)(2,1)}, f32[1,768]{1,0:T(1,128)S(1)}, f32[1,768]{1,0:T(1,128)}, f32[1,768,128]{2,1,0:T(8,128)}, /*in...) while((s32[]{:T(128)}, bf16[2,2304,128]{2,1,0:T(8,128)(2,1)}, ...), condition=%wide.region_14.15_spmd, body=%wide.region_7.14_spmd.sunk | while | flops 929181184 | bytes 57951692 | solution.py:187
  72.2 7.2 %collective-permute-start = (bf16[2,2304,128]{2,1,0:T(8,128)(2,1)}, bf16[2,2304,128]{2,1,0:T(8,128)(2,1)S(1)}, u32[]{:S(2)}, u32[]{:S(2)}) collective-permute-start(bf16[2,2304,128]{2,1,0:T(8,128)(2,1)} %get-tuple-element.428), channel_id=1, source_target_pairs={{0,32},{8,40},{16,48},{24,56},{32,64},{40,72},{48,80},{56,88},{64,... | collective-permute-start | bytes 3538952 | tf_op jit(solution)/shard_map/while/body/eval_jaxpr/ppermute | solution.py:14
  81.2 48.9 %collective-permute-done = bf16[2,2304,128]{2,1,0:T(8,128)(2,1)S(1)} collective-permute-done((bf16[2,2304,128]{2,1,0:T(8,128)(2,1)}, bf16[2,2304,128]{2,1,0:T(8,128)(2,1)S(1)}, u32[]{:S(2)}, u32[]{:S(2)}) %collective-permute-start) | collective-permute-done | bytes 1179680 | tf_op jit(solution)/shard_map/while/body/eval_jaxpr/ppermute | solution.py:14
  130.2 2.1 fusion.104
  134.9 1.6 fusion.107
  138.9 3.2 scatter_custom_fusion.14
  142.1 3.2 scatter_custom_fusion.15
  145.3 5.2 fusion.108
  150.5 6.3 collective-permute-start
  158.7 44.1 %collective-permute-done = bf16[2,2304,128]{2,1,0:T(8,128)(2,1)S(1)} collective-permute-done((bf16[2,2304,128]{2,1,0:T(8,128)(2,1)}, bf16[2,2304,128]{2,1,0:T(8,128)(2,1)S(1)}, u32[]{:S(2)}, u32[]{:S(2)}) %collective-permute-start) | collective-permute-done | bytes 1179680 | tf_op jit(solution)/shard_map/while/body/eval_jaxpr/ppermute | solution.py:14
  202.7 2.1 fusion.104
  207.5 1.6 fusion.107
  211.5 3.2 scatter_custom_fusion.14
  214.7 3.2 scatter_custom_fusion.15
  217.9 5.2 fusion.108
  223.1 5.1 collective-permute-start
  230.0 45.0 %collective-permute-done = bf16[2,2304,128]{2,1,0:T(8,128)(2,1)S(1)} collective-permute-done((bf16[2,2304,128]{2,1,0:T(8,128)(2,1)}, bf16[2,2304,128]{2,1,0:T(8,128)(2,1)S(1)}, u32[]{:S(2)}, u32[]{:S(2)}) %collective-permute-start) | collective-permute-done | bytes 1179680 | tf_op jit(solution)/shard_map/while/body/eval_jaxpr/ppermute | solution.py:14
  275.0 2.1 fusion.104
  279.8 1.6 fusion.107
  283.8 3.2 scatter_custom_fusion.14
  287.0 3.2 scatter_custom_fusion.15
  290.2 5.2 fusion.108
  295.3 3.3 collective-permute-start
  300.5 35.3 %collective-permute-done = bf16[2,2304,128]{2,1,0:T(8,128)(2,1)S(1)} collective-permute-done((bf16[2,2304,128]{2,1,0:T(8,128)(2,1)}, bf16[2,2304,128]{2,1,0:T(8,128)(2,1)S(1)}, u32[]{:S(2)}, u32[]{:S(2)}) %collective-permute-start) | collective-permute-done | bytes 1179680 | tf_op jit(solution)/shard_map/while/body/eval_jaxpr/ppermute | solution.py:14
  335.8 2.1 fusion.104
  340.6 1.6 fusion.107
  344.6 3.2 scatter_custom_fusion.14
  347.8 3.2 scatter_custom_fusion.15
  351.0 5.2 fusion.108
  356.2 6.3 collective-permute-start
  364.4 49.2 %collective-permute-done = bf16[2,2304,128]{2,1,0:T(8,128)(2,1)S(1)} collective-permute-done((bf16[2,2304,128]{2,1,0:T(8,128)(2,1)}, bf16[2,2304,128]{2,1,0:T(8,128)(2,1)S(1)}, u32[]{:S(2)}, u32[]{:S(2)}) %collective-permute-start) | collective-permute-done | bytes 1179680 | tf_op jit(solution)/shard_map/while/body/eval_jaxpr/ppermute | solution.py:14
  413.6 2.1 fusion.104
  418.4 1.6 fusion.107
  422.4 3.2 scatter_custom_fusion.14
  425.6 3.2 scatter_custom_fusion.15
  428.8 5.2 fusion.108
  435.8 53.5 %collective-permute-done = bf16[2,2304,128]{2,1,0:T(8,128)(2,1)S(1)} collective-permute-done((bf16[2,2304,128]{2,1,0:T(8,128)(2,1)}, bf16[2,2304,128]{2,1,0:T(8,128)(2,1)S(1)}, u32[]{:S(2)}, u32[]{:S(2)}) %collective-permute-start) | collective-permute-done | bytes 1179680 | tf_op jit(solution)/shard_map/while/body/eval_jaxpr/ppermute | solution.py:14
  489.3 2.1 fusion.104
  498.1 3.2 scatter_custom_fusion.14
  501.3 3.2 scatter_custom_fusion.15
  504.5 5.2 fusion.108
  512.1 44.1 %collective-permute-done = bf16[2,2304,128]{2,1,0:T(8,128)(2,1)S(1)} collective-permute-done((bf16[2,2304,128]{2,1,0:T(8,128)(2,1)}, bf16[2,2304,128]{2,1,0:T(8,128)(2,1)S(1)}, u32[]{:S(2)}, u32[]{:S(2)}) %collective-permute-start) | collective-permute-done | bytes 1179680 | tf_op jit(solution)/shard_map/while/body/eval_jaxpr/ppermute | solution.py:14
  556.1 2.1 fusion.104
  564.9 3.2 scatter_custom_fusion.14
  568.1 3.2 scatter_custom_fusion.15
  571.3 5.2 fusion.108
  578.5 2.2 convolution_convert_fusion
  580.7 81.7 %all-reduce.2.cloned.1.call-done = bf16[256,3072]{1,0:T(8,128)(2,1)} async-done(((bf16[256,3072]{1,0:T(8,128)(2,1)}), bf16[256,3072]{1,0:T(8,128)(2,1)}) %all-reduce.2.cloned.1.call-update) | async-done | bytes 1572880 | tf_op jit(solution)/shard_map/psum | solution.py:198
  662.4 1.6 convert_convert_fusion
  (198 shorter events, 70.8 us)
Async XLA Ops:
  7.2 571.3 %copy-start = (bf16[384,3072]{1,0:T(8,128)(2,1)S(1)}, bf16[384,3072]{1,0:T(8,128)(2,1)}, u32[]{:S(2)}) copy-start(bf16[384,3072]{1,0:T(8,128)(2,1)} %param.17) | copy-start | bytes 7077892
  8.4 41.2 %copy-start.4 = (bf16[2048,128]{1,0:T(8,128)(2,1)}, bf16[2048,128]{1,0:T(8,128)(2,1)S(1)}, u32[]{:S(2)}) copy-start(bf16[2048,128]{1,0:T(8,128)(2,1)S(1)} %copy.66) | copy-start | bytes 1572868
  8.4 8.9 %copy-start.15 = (s32[4]{0:T(128)S(1)}, s32[4]{0:T(128)}, u32[]{:S(2)}) copy-start(s32[4]{0:T(128)} %param.21) | copy-start | bytes 52
  8.4 9.5 %copy-start.16 = (s32[4]{0:T(128)S(1)}, s32[4]{0:T(128)}, u32[]{:S(2)}) copy-start(s32[4]{0:T(128)} %param.20) | copy-start | bytes 52
  8.4 10.1 %copy-start.9 = (f32[3072]{0:T(1024)S(1)}, f32[3072]{0:T(1024)}, u32[]{:S(2)}) copy-start(f32[3072]{0:T(1024)} %param.13) | copy-start | bytes 36868
  12.7 26.2 %all-to-all-start = ((bf16[8,256,384]{2,1,0:T(8,128)(2,1)}), bf16[8,256,384]{2,1,0:T(8,128)(2,1)}, u32[]{:S(2)}, u32[]{:S(2)}) async-start(bf16[8,256,384]{2,1,0:T(8,128)(2,1)} %stack.8), calls=%async_computation | async-start | bytes 3145728 | tf_op jit(solution)/shard_map/all_to_all | solution.py:47
  17.2 645.2 %all-reduce.2.cloned.1.call-start = ((), (), s32[]{:S(2)}) async-start(), calls=%async_computation.1 | async-start | bytes 3145728 | tf_op jit(solution)/shard_map/psum | solution.py:198
  24.0 21.2 %copy-start.11 = (s32[256]{0:T(256)}, s32[256]{0:T(256)S(1)}, u32[]{:S(2)}) copy-start(s32[256]{0:T(256)S(1)} %get-tuple-element.315) | copy-start | bytes 3076
  41.4 5.0 copy-start.14
  43.4 3.9 copy-start.13
  45.3 1.2 copy-start.2
  58.3 2.1 copy-start.3
  58.3 2.9 copy-start.5
  58.3 2.9 copy-start.6
  60.3 3.4 copy-start.10
  63.8 2.1 copy-start.12
  72.2 58.0 %collective-permute-start = (bf16[2,2304,128]{2,1,0:T(8,128)(2,1)}, bf16[2,2304,128]{2,1,0:T(8,128)(2,1)S(1)}, u32[]{:S(2)}, u32[]{:S(2)}) collective-permute-start(bf16[2,2304,128]{2,1,0:T(8,128)(2,1)} %get-tuple-element.428), channel_id=1, source_target_pairs={{0,32},{8,40},{16,48},{24,56},{32,64},{40,72},{48,80},{56,88},{64,... | collective-permute-start | bytes 3538952 | tf_op jit(solution)/shard_map/while/body/eval_jaxpr/ppermute | solution.py:14
  132.2 4.2 copy-start.1
  134.9 1.8 copy-start.7
  136.7 1.2 copy-start.8
  150.5 52.3 %collective-permute-start = (bf16[2,2304,128]{2,1,0:T(8,128)(2,1)}, bf16[2,2304,128]{2,1,0:T(8,128)(2,1)S(1)}, u32[]{:S(2)}, u32[]{:S(2)}) collective-permute-start(bf16[2,2304,128]{2,1,0:T(8,128)(2,1)} %get-tuple-element.428), channel_id=1, source_target_pairs={{0,32},{8,40},{16,48},{24,56},{32,64},{40,72},{48,80},{56,88},{64,... | collective-permute-start | bytes 3538952 | tf_op jit(solution)/shard_map/while/body/eval_jaxpr/ppermute | solution.py:14
  204.8 4.2 copy-start.1
  207.5 1.8 copy-start.7
  209.3 1.2 copy-start.8
  223.1 52.0 %collective-permute-start = (bf16[2,2304,128]{2,1,0:T(8,128)(2,1)}, bf16[2,2304,128]{2,1,0:T(8,128)(2,1)S(1)}, u32[]{:S(2)}, u32[]{:S(2)}) collective-permute-start(bf16[2,2304,128]{2,1,0:T(8,128)(2,1)} %get-tuple-element.428), channel_id=1, source_target_pairs={{0,32},{8,40},{16,48},{24,56},{32,64},{40,72},{48,80},{56,88},{64,... | collective-permute-start | bytes 3538952 | tf_op jit(solution)/shard_map/while/body/eval_jaxpr/ppermute | solution.py:14
  277.1 4.2 copy-start.1
  279.8 1.8 copy-start.7
  281.6 1.2 copy-start.8
  295.3 40.5 %collective-permute-start = (bf16[2,2304,128]{2,1,0:T(8,128)(2,1)}, bf16[2,2304,128]{2,1,0:T(8,128)(2,1)S(1)}, u32[]{:S(2)}, u32[]{:S(2)}) collective-permute-start(bf16[2,2304,128]{2,1,0:T(8,128)(2,1)} %get-tuple-element.428), channel_id=1, source_target_pairs={{0,32},{8,40},{16,48},{24,56},{32,64},{40,72},{48,80},{56,88},{64,... | collective-permute-start | bytes 3538952 | tf_op jit(solution)/shard_map/while/body/eval_jaxpr/ppermute | solution.py:14
  337.9 4.2 copy-start.1
  340.6 1.8 copy-start.7
  342.4 1.2 copy-start.8
  356.2 57.5 %collective-permute-start = (bf16[2,2304,128]{2,1,0:T(8,128)(2,1)}, bf16[2,2304,128]{2,1,0:T(8,128)(2,1)S(1)}, u32[]{:S(2)}, u32[]{:S(2)}) collective-permute-start(bf16[2,2304,128]{2,1,0:T(8,128)(2,1)} %get-tuple-element.428), channel_id=1, source_target_pairs={{0,32},{8,40},{16,48},{24,56},{32,64},{40,72},{48,80},{56,88},{64,... | collective-permute-start | bytes 3538952 | tf_op jit(solution)/shard_map/while/body/eval_jaxpr/ppermute | solution.py:14
  415.7 4.2 copy-start.1
  418.4 1.8 copy-start.7
  420.2 1.2 copy-start.8
  433.9 55.4 %collective-permute-start = (bf16[2,2304,128]{2,1,0:T(8,128)(2,1)}, bf16[2,2304,128]{2,1,0:T(8,128)(2,1)S(1)}, u32[]{:S(2)}, u32[]{:S(2)}) collective-permute-start(bf16[2,2304,128]{2,1,0:T(8,128)(2,1)} %get-tuple-element.428), channel_id=1, source_target_pairs={{0,32},{8,40},{16,48},{24,56},{32,64},{40,72},{48,80},{56,88},{64,... | collective-permute-start | bytes 3538952 | tf_op jit(solution)/shard_map/while/body/eval_jaxpr/ppermute | solution.py:14
  491.4 4.2 copy-start.1
  494.1 1.8 copy-start.7
  495.9 1.2 copy-start.8
  509.6 46.5 %collective-permute-start = (bf16[2,2304,128]{2,1,0:T(8,128)(2,1)}, bf16[2,2304,128]{2,1,0:T(8,128)(2,1)S(1)}, u32[]{:S(2)}, u32[]{:S(2)}) collective-permute-start(bf16[2,2304,128]{2,1,0:T(8,128)(2,1)} %get-tuple-element.428), channel_id=1, source_target_pairs={{0,32},{8,40},{16,48},{24,56},{32,64},{40,72},{48,80},{56,88},{64,... | collective-permute-start | bytes 3538952 | tf_op jit(solution)/shard_map/while/body/eval_jaxpr/ppermute | solution.py:14
  558.2 4.2 copy-start.1
  560.9 1.8 copy-start.7
  562.7 1.2 copy-start.8
Sparse Core Ops, SparseCore 0:
  580.8 81.5 all-reduce.1
